TPU v7x, 256 devices: a whole 4x4x8 slice. The times are simulated.
256 devices in a mesh: seq: 32 (over z, y), mp: 4 (over x), req: 2 (over core).
Axes of the slice: x: 4, y: 4, z: 8, core: 2. Of those that a mesh axis runs over, the one named last changes fastest.
Arguments:
- hidden: bfloat16 [2, 8192, 3072], P('req', 'seq', 'mp'), may hold values from -6 to 6
- norm_gain: bfloat16 [3072], replicated, may hold values from 0.5 to 1.5
- w_query: bfloat16 [3072, 1024], P(None, 'mp'), may hold values from -0.109375 to 0.109375
- w_keyval: bfloat16 [3072, 512], P(None, 'mp'), may hold values from -0.109375 to 0.109375
- w_attn_out: bfloat16 [1024, 3072], P('mp'), may hold values from -1.5 to 1.5
- w_inner: bfloat16 [3072, 2, 1536], P(None, None, 'mp'), may hold values from -0.109375 to 0.109375
- w_bc: bfloat16 [3072, 512], P(None, 'mp'), may hold values from -0.109375 to 0.109375
- w_dt: bfloat16 [3072, 12], P(None, 'mp'), may hold values from -0.109375 to 0.109375
- dt_bias: float32 [12], P('mp'), may hold values from -4 to 0
- a_log: float32 [12], P('mp'), may hold values from -12 to 0
- d_skip: float32 [12], P('mp'), may hold values from 0.1 to 10
- conv_x: bfloat16 [4, 1536], P(None, 'mp'), may hold values from -3 to 3
- conv_bc: bfloat16 [4, 512], replicated, may hold values from -3 to 3
- mamba_gain: bfloat16 [1536], P('mp'), may hold values from 0.5 to 1.5
- w_mamba_out: bfloat16 [1536, 3072], P('mp'), may hold values from -0.15625 to 0.15625
- cache: bfloat16 [2, 8192, 512], P('req', 'seq', 'mp'), may hold values from -70 to 70, as said below
- cache_len: int32 [2], P('req'), may hold values from 256 to 8192
- tail_x: bfloat16 [2, 3, 1536], P('req', None, 'mp'), may hold values from -6 to 6
- tail_bc: bfloat16 [2, 3, 512], P('req'), may hold values from -6 to 6
- ssm_init: float32 [2, 12, 128, 256], P('req', 'mp'), may hold values from -6 to 6
Outputs:
- layer_out: bfloat16 [2, 8192, 3072], P('req', 'seq', 'mp')
- new_keyval: bfloat16 [2, 8192, 512], P('req', 'seq', 'mp')
- block_states: float32 [2, 32, 12, 128, 256], P('req', 'seq', 'mp')
Inputs may be any that keep to these rules, and one draw needn't show every extreme that they name: Rows of the cache at or past cache_len are unused.
All inputs are finite; a program needn't handle non-finite values.
Results may differ from a plain program's by a relative error of at most 0.0097.
Values may be sent and summed in bfloat16 or wider, within the bound.
A program may use at most 192 MiB of HBM per device.

v0:
```python
import jax
import jax.numpy as jnp
from jax import lax
from jax.sharding import PartitionSpec as P

HD = 128
QH = 8
KVH = 2
NS = 256
CONV = 4
epsilon = 1e-05
rope_base = 100000000000.0
negative = -1e30


def shifted(block, axis, distance):
    devices = range(lax.axis_size(axis))
    route = [(i - distance, i) for i in devices if i - distance in devices]
    return lax.ppermute(block, axis, route)


def prefix(part, axis, combine, identity):
    place = lax.axis_index(axis)
    gathered = jax.tree.map(lambda a: lax.all_gather(a, axis), part)
    state = jax.tree.map(lambda a, e: jnp.zeros_like(a) + jnp.asarray(e, a.dtype), part, identity)

    def one(turn, state):
        return combine(
            state, jax.tree.map(lambda a: lax.dynamic_index_in_dim(a, turn, 0, False), gathered)
        )

    return lax.fori_loop(0, place, one, state)


def rotate(values, positions):
    half = HD // 2
    freqs = rope_base ** (-jnp.arange(half, dtype=jnp.float32) * 2.0 / HD)
    angles = positions.astype(jnp.float32)[:, None] * freqs[None, :]
    cosine = jnp.cos(angles)[:, None, :]
    sine = jnp.sin(angles)[:, None, :]
    first = values[..., :half]
    second = values[..., half:]
    return jnp.concatenate(
        [first * cosine - second * sine, second * cosine + first * sine], axis=-1
    )


def rms_scale(values):
    mean_sq = jnp.mean(values * values, axis=-1, keepdims=True)
    return values * lax.rsqrt(mean_sq + epsilon)


def causal_conv(tail, inputs, taps):
    padded = jnp.concatenate([tail, inputs], axis=0).astype(jnp.float32)
    count = inputs.shape[0]
    total = jnp.zeros(inputs.shape, jnp.float32)
    for offset in range(CONV):
        total = total + taps[offset].astype(jnp.float32)[None, :] * padded[offset : offset + count]
    return jax.nn.silu(total)


def join_states(earlier, later):
    return (earlier[0] * later[0], later[0][:, None, None] * earlier[1] + later[1])


def shards(
    hidden,
    norm_gain,
    w_query,
    w_keyval,
    w_attn_out,
    w_inner,
    w_bc,
    w_dt,
    dt_bias,
    a_log,
    d_skip,
    conv_x,
    conv_bc,
    mamba_gain,
    w_mamba_out,
    cache,
    cache_len,
    tail_x,
    tail_bc,
    ssm_init,
):
    high = lax.Precision.HIGHEST
    own_rows = hidden[0]
    tokens = own_rows.shape[0]
    seq_pos = lax.axis_index("seq")
    mp_pos = lax.axis_index("mp")
    length = cache_len[0]
    whole = lax.all_gather(own_rows, "mp", axis=1, tiled=True)
    normed = (rms_scale(whole.astype(jnp.float32)) * norm_gain.astype(jnp.float32)).astype(
        jnp.bfloat16
    )
    positions = length + seq_pos * tokens + jnp.arange(tokens, dtype=jnp.int32)
    local_heads = w_query.shape[1] // HD
    query = rotate(
        jnp.dot(normed, w_query, preferred_element_type=jnp.float32).reshape(
            tokens, local_heads, HD
        ),
        positions,
    ).astype(jnp.bfloat16)
    projected = jnp.dot(normed, w_keyval, preferred_element_type=jnp.float32)
    roped = rotate(projected[:, None, :], positions)[:, 0, :]
    kv_block = jnp.where(mp_pos % 2 == 0, roped, projected).astype(jnp.bfloat16)
    bc_block = jnp.dot(normed, w_bc, preferred_element_type=jnp.float32).astype(jnp.bfloat16)
    bc_all = lax.all_gather(bc_block, "mp", axis=1, tiled=True)
    mp_size = lax.axis_size("mp")
    pairs_of = [(i, i ^ 1) for i in range(mp_size)]
    is_key_block = mp_pos % 2 == 0

    def paired(own):
        other = lax.ppermute(own, "mp", pairs_of)
        return jnp.where(
            is_key_block,
            jnp.concatenate([own, other], axis=1),
            jnp.concatenate([other, own], axis=1),
        )

    cache_all = lax.all_gather(paired(cache[0]), "seq", axis=0, tiled=True)
    new_all = lax.all_gather(paired(kv_block), "seq", axis=0, tiled=True)
    inner = jnp.einsum("td,dkc->tkc", normed, w_inner, preferred_element_type=jnp.float32).astype(
        jnp.bfloat16
    )
    rim = CONV - 1
    prev_x, prev_bc = shifted((inner[tokens - rim :, 1], bc_all[tokens - rim :]), "seq", 1)
    first_block = seq_pos == 0
    prev_x = jnp.where(first_block, tail_x[0], prev_x)
    prev_bc = jnp.where(first_block, tail_bc[0], prev_bc)
    mamba_heads = dt_bias.shape[0]
    x_conv = causal_conv(prev_x, inner[:, 1], conv_x).reshape(tokens, mamba_heads, HD)
    bc_conv = causal_conv(prev_bc, bc_all, conv_bc)
    b_mat = bc_conv[:, :NS]
    c_mat = bc_conv[:, NS:]
    step_size = jax.nn.softplus(jnp.dot(normed, w_dt, preferred_element_type=jnp.float32) + dt_bias)
    log_decay = -step_size * jnp.exp(a_log)[None, :]
    cumulative = jnp.cumsum(log_decay, axis=0)
    pairs = jnp.dot(c_mat, b_mat.T, precision=high)
    gap = cumulative[:, None, :] - cumulative[None, :, :]
    token_ids = jnp.arange(tokens)
    lower = (token_ids[:, None] >= token_ids[None, :])[:, :, None]
    decay = jnp.where(lower, jnp.exp(jnp.where(lower, gap, 0.0)), 0.0)
    mixing = decay * pairs[:, :, None] * step_size[None, :, :]
    inner_out = jnp.einsum("tsh,shp->thp", mixing, x_conv, precision=high)
    to_end = jnp.exp(cumulative[-1][None, :] - cumulative) * step_size
    own_state = jnp.einsum("sh,shp,sn->hpn", to_end, x_conv, b_mat, precision=high)
    block_decay = jnp.exp(cumulative[-1])
    seq_size = lax.axis_size("seq")
    rows = HD // seq_size
    pieces = jnp.transpose(own_state.reshape(mamba_heads, seq_size, rows, NS), (1, 0, 2, 3))
    decays = jnp.broadcast_to(block_decay[None, :, None, None], (seq_size, mamba_heads, 1, NS))
    columns = lax.all_to_all(jnp.concatenate([pieces, decays], axis=2), "seq", 0, 0, tiled=True)
    carry = lax.dynamic_slice_in_dim(ssm_init[0], seq_pos * rows, rows, 1)
    entering = []
    for source in range(seq_size):
        entering.append(carry)
        part = columns[source]
        carry = part[:, rows:, :] * carry + part[:, :rows, :]
    entering = lax.all_to_all(jnp.stack(entering, axis=0), "seq", 0, 0, tiled=True)
    incoming = jnp.transpose(entering, (1, 0, 2, 3)).reshape(mamba_heads, HD, NS)
    carried = jnp.exp(cumulative)[:, :, None] * jnp.einsum(
        "tn,hpn->thp", c_mat, incoming, precision=high
    )
    mamba_y = inner_out + carried + d_skip[None, :, None] * x_conv
    state_after = block_decay[:, None, None] * incoming + own_state
    gated = mamba_y * jax.nn.silu(inner[:, 0].astype(jnp.float32).reshape(tokens, mamba_heads, HD))
    mixed = (
        rms_scale(gated).reshape(tokens, mamba_heads * HD) * mamba_gain.astype(jnp.float32)
    ).astype(jnp.bfloat16)
    cache_rows = cache.shape[1]
    shard_rows = cache_rows + tokens
    group = mp_pos * local_heads // (QH // KVH)
    query_index = seq_pos * tokens + jnp.arange(tokens, dtype=jnp.int32)
    scale = 1.0 / float(HD) ** 0.5
    piece = jnp.concatenate([cache_all, new_all], axis=0)
    top = jnp.full((local_heads, tokens), negative, jnp.float32)
    total_cache = cache_all.shape[0]
    index = jnp.arange(piece.shape[0], dtype=jnp.int32)
    in_cache = index < total_cache
    slot_ok = in_cache & (index < length)
    new_index = index - total_cache
    valid = slot_ok[None, :] | (~in_cache)[None, :] & (new_index[None, :] <= query_index[:, None])
    scores = (
        jnp.einsum("qhd,kd->hqk", query, piece[:, :HD], preferred_element_type=jnp.float32) * scale
    )
    masked = jnp.where(valid[None], scores, negative)
    new_top = jnp.maximum(top, jnp.max(masked, axis=-1))
    weights = jnp.where(valid[None], jnp.exp(masked - new_top[:, :, None]), 0.0)
    total = jnp.sum(weights, axis=-1)
    accum = jnp.einsum(
        "hqk,kd->hqd",
        weights.astype(jnp.bfloat16),
        piece[:, HD : 2 * HD],
        preferred_element_type=jnp.float32,
    )
    top, total, accum = (new_top, total, accum)
    attended = jnp.transpose(accum / total[:, :, None], (1, 0, 2)).reshape(tokens, local_heads * HD)
    attended = attended.astype(jnp.bfloat16)
    term = jnp.dot(attended, w_attn_out, preferred_element_type=jnp.float32)
    term = term + jnp.dot(mixed, w_mamba_out, preferred_element_type=jnp.float32)
    summed = lax.psum_scatter(term, "mp", scatter_dimension=1, tiled=True)
    layer = (summed + own_rows.astype(jnp.float32)).astype(jnp.bfloat16)
    return (layer[None], kv_block[None], state_after[None, None])


def solution(mesh):
    placed = (
        P("req", "seq", "mp"),
        P(),
        P(None, "mp"),
        P(None, "mp"),
        P("mp", None),
        P(None, None, "mp"),
        P(None, "mp"),
        P(None, "mp"),
        P("mp"),
        P("mp"),
        P("mp"),
        P(None, "mp"),
        P(),
        P("mp"),
        P("mp", None),
        P("req", "seq", "mp"),
        P("req"),
        P("req", None, "mp"),
        P("req", None, None),
        P("req", "mp", None, None),
    )
    return jax.shard_map(
        shards,
        mesh=mesh,
        in_specs=placed,
        out_specs=(P("req", "seq", "mp"), P("req", "seq", "mp"), P("req", "seq", "mp", None, None)),
        check_vma=False,
    )
```

profile of v0, /device:TPU:1, one launch (start us, length us, event | category | flops | bytes accessed | tf_op | source)
XLA Modules:
  0.0 330.6 jit_solution(8155268910153722102)
XLA Ops:
  8.0 0.9 copy.66
  8.9 2.1 collective-permute-start
  14.5 0.9 convert_reduce_fusion.3
  15.4 0.8 slice_convert_fusion.4
  16.8 1.3 multiply_cosine_fusion
  18.8 15.6 %and_or_fusion = pred[256,16384]{0,1:T(8,128)(4,1)} fusion(s32[256]{0:T(256)S(1)} %iota_add_fusion.1, s32[16384]{0:T(1024)S(1)} %iota_add_fusion, pred[16384]{0:T(1024)(128)(4,1)S(1)} %get-tuple-element.103, pred[16384]{0:T(1024)(128)(4,1)S(1)} %get-tuple-element.104), kind=kLoop, calls=%fused_computation.7 | loop fusion | flops 12582912 | bytes 4293632 | tf_op jit(solution)/shard_map/or | solution.py:185
  34.4 8.3 %all-gather.9.cloned.1.call-done = bf16[1,256,3072]{2,1,0:T(8,128)(2,1)} async-done(((bf16[1,256,768]{2,1,0:T(8,128)(2,1)}), bf16[1,256,3072]{2,1,0:T(8,128)(2,1)}) %all-gather.9.cloned.1.call-update) | async-done | bytes 1572880 | tf_op jit(solution)/shard_map/all_gather | solution.py:94
  42.7 1.8 fusion.9
  44.5 1.9 fusion.11
  46.4 1.1 copy-done.1
  48.1 0.9 reduce-window.6
  49.5 4.3 %fusion.13 = bf16[256,2,384]{2,0,1:T(8,128)(2,1)S(1)} fusion(bf16[3072,2,384]{2,1,0:T(2,128)(2,1)} %param.25, bf16[256,3072]{1,0:T(8,128)(2,1)} %copy-done.1), kind=kOutput, calls=%fused_computation.20 | convolution fusion | flops 1208156160 | bytes 6684672 | tf_op jit(solution)/shard_map/td,dkc->tkc/dot_general | solution.py:125
  53.9 3.1 collective-permute-start.2
  58.6 9.8 %all_gather.15 = bf16[256,512]{1,0:T(8,128)(2,1)S(1)} all-gather(bf16[256,128]{1,0:T(8,128)(2,1)S(1)} %convolution_convert_fusion), channel_id=1, replica_groups=mesh['seq'=32,'mp'=4,'req'=2] {'mp'}, dimensions={1}, use_global_device_ids=true | all-gather | bytes 327680 | tf_op jit(solution)/shard_map/all_gather | solution.py:110
  68.4 2.7 collective-permute-start.3
  71.5 0.9 copy.72
  72.8 1.5 fusion.45
  74.7 1.0 pad_maximum_fusion
  75.7 10.7 %all-to-all-start = ((f32[32,3,5,256]{3,1,2,0:T(4,128)}), f32[32,3,5,256]{3,1,2,0:T(4,128)}, u32[]{:S(2)}, u32[]{:S(2)}) async-start(f32[32,3,5,256]{3,1,2,0:T(4,128)} %pad_maximum_fusion), calls=%async_computation | async-start | bytes 1310720 | tf_op jit(solution)/shard_map/all_to_all | solution.py:155
  86.5 2.3 fusion.90
  89.1 1.0 collective-permute-start.1
  90.8 1.5 collective-permute-done.1
  93.0 8.7 %all-to-all-done = f32[32,3,5,256]{3,1,2,0:T(4,128)} async-done(((f32[32,3,5,256]{3,1,2,0:T(4,128)}), f32[32,3,5,256]{3,1,2,0:T(4,128)}, u32[]{:S(2)}, u32[]{:S(2)}) %all-to-all-start) | async-done | bytes 491552 | tf_op jit(solution)/shard_map/all_to_all | solution.py:155
  101.8 0.9 slice_bitcast_fusion.30
  102.8 1.0 slice_bitcast_fusion.11
  122.8 1.9 copy.77
  124.7 7.0 %all-to-all-start.1 = ((f32[32,3,4,256]{3,2,1,0:T(4,128)}), f32[32,3,4,256]{3,2,1,0:T(4,128)}, u32[]{:S(2)}, u32[]{:S(2)}) async-start(f32[32,3,4,256]{3,2,1,0:T(4,128)} %copy.77), calls=%async_computation.1 | async-start | bytes 786432 | tf_op jit(solution)/shard_map/all_to_all | solution.py:162
  132.0 2.6 fusion.91
  135.3 1.0 copy.86
  136.3 1.9 copy.79
  138.2 1.7 copy.85
  140.0 1.8 subtract_convert_fusion
  142.2 1.4 all-to-all-done.1
  143.6 1.8 copy.78
  145.3 1.9 reshape.277
  147.2 1.5 convolution_multiply_fusion
  148.7 2.5 multiply_reduce_fusion
  151.4 4.6 %constant_dynamic-update-slice_fusion.1 = bf16[16384,256]{0,1:T(8,128)(2,1)} fusion(bf16[8192,256]{0,1:T(8,128)(2,1)} %all-gather.5.cloned.1.call-done), kind=kLoop, calls=%fused_computation.102 | loop fusion | bytes 8388608
  156.0 62.0 %all-gather.7.cloned.1.call-done = bf16[8192,256]{0,1:T(8,128)(2,1)} async-done(((bf16[256,256]{0,1:T(8,128)(2,1)}), bf16[8192,256]{0,1:T(8,128)(2,1)}) %all-gather.7.cloned.1.call-update) | async-done | bytes 4194320 | tf_op jit(solution)/shard_map/all_gather | solution.py:124
  218.0 4.6 %constant_dynamic-update-slice_fusion = bf16[16384,256]{0,1:T(8,128)(2,1)} fusion(bf16[16384,256]{0,1:T(8,128)(2,1)} %constant_dynamic-update-slice_fusion.1, bf16[8192,256]{0,1:T(8,128)(2,1)} %all-gather.7.cloned.1.call-done), kind=kLoop, calls=%fused_computation.101 | loop fusion | bytes 8388608 | tf_op jit(solution)/shard_map/concatenate | solution.py:178
  222.6 17.3 %fusion = (f32[2,256]{1,0:T(2,128)S(1)}, f32[16384,256,2]{1,0,2:T(8,128)}) fusion(pred[256,16384]{0,1:T(8,128)(4,1)} %and_or_fusion, bf16[256,2,64]{2,0,1:T(8,128)(2,1)S(1)} %copy-done.8, bf16[256,2,64]{2,0,1:T(8,128)(2,1)S(1)} %copy-done.7, bf16[16384,256]{0,1:T(8,128)(2,1)} %constant_dynamic-update-slice_fusion), kind=kOutput, calls=%fused_computation.2 | convolution fusion | flops 2172911104 | bytes 42076160 | tf_op jit(solution)/shard_map/qhd,kd->hqk/dot_general | solution.py:187
  239.9 15.7 %fusion.1 = f32[2,256]{1,0:T(2,128)S(1)} fusion(f32[16384,256,2]{1,0,2:T(8,128)} %get-tuple-element.98, f32[2,256]{1,0:T(2,128)S(1)} %broadcast_maximum_fusion, pred[256,16384]{0,1:T(8,128)(4,1)} %and_or_fusion), kind=kLoop, calls=%fused_computation.3 | loop fusion | flops 41942528 | bytes 37752832 | tf_op jit(solution)/shard_map/reduce_sum | solution.py:192
  255.6 17.2 %fusion.27 = bf16[256,2,128]{0,2,1:T(8,128)(2,1)S(1)} fusion(f32[16384,256,2]{1,0,2:T(8,128)} %get-tuple-element.98, f32[2,256]{1,0:T(2,128)S(1)} %broadcast_maximum_fusion, pred[256,16384]{0,1:T(8,128)(4,1)} %and_or_fusion, bf16[16384,256]{0,1:T(8,128)(2,1)} %constant_dynamic-update-slice_fusion, f32[256,2]{0,1:T(2,128)S(1)} %bitcast.367), kind=kOutput, calls=%fused_computation.30 | convolution fusion | flops 2189557760 | bytes 42078208 | tf_op jit(solution)/shard_map/hqk,kd->hqd/dot_general | solution.py:193
  272.8 2.0 fusion.92
  274.9 2.7 convolution_add_fusion
  278.4 0.9 add_bitcast_fusion
  279.2 42.8 %reduce-scatter.2.cloned.1.call-done = f32[256,768]{1,0:T(8,128)} async-done(((f32[256,3072]{1,0:T(8,128)}), f32[256,768]{1,0:T(8,128)}) %reduce-scatter.2.cloned.1.call-update) | async-done | bytes 786448 | tf_op jit(solution)/shard_map/reduce_scatter | solution.py:204
  322.0 2.0 fusion.40
  (135 shorter events, 31.5 us)
Async XLA Ops:
  7.2 267.7 %copy-start = (bf16[384,3072]{1,0:T(8,128)(2,1)S(1)}, bf16[384,3072]{1,0:T(8,128)(2,1)}, u32[]{:S(2)}) copy-start(bf16[384,3072]{1,0:T(8,128)(2,1)} %param.34) | copy-start | bytes 7077892
  7.2 35.5 %all-gather.9.cloned.1.call-start = ((), (), s32[]{:S(2)}) async-start(), calls=%async_computation.6 | async-start | bytes 1966080 | tf_op jit(solution)/shard_map/all_gather | solution.py:94
  7.9 143.5 %all-gather.5.cloned.1.call-start = ((), (), s32[]{:S(2)}) async-start(), calls=%async_computation.3 | async-start | bytes 4325376 | tf_op jit(solution)/shard_map/all_gather | solution.py:123
  8.9 9.2 %collective-permute-start = (bf16[256,128]{0,1:T(8,128)(2,1)S(1)}, bf16[256,128]{0,1:T(8,128)(2,1)S(1)}, u32[]{:S(2)}, u32[]{:S(2)}) collective-permute-start(bf16[256,128]{0,1:T(8,128)(2,1)S(1)} %bitcast.357), channel_id=1, source_target_pairs={{0,2},{2,0},{4,6},{6,4},{1,3},{3,1},{5,7},{7,5},{8,10},{10,8},{12,... | collective-permute-start | bytes 196616 | tf_op jit(solution)/shard_map/ppermute | solution.py:116
  18.8 28.8 %copy-start.9 = (bf16[3072,3]{0,1:T(4,128)(2,1)S(1)}, bf16[3072,3]{0,1:T(4,128)(2,1)}, u32[]{:S(2)}) copy-start(bf16[3072,3]{0,1:T(4,128)(2,1)} %param.27) | copy-start | bytes 55300
  18.8 28.8 %copy-start.14 = (f32[3]{0:T(128)S(1)}, f32[3]{0:T(128)}, u32[]{:S(2)}) copy-start(f32[3]{0:T(128)} %param.28) | copy-start | bytes 40
  46.4 1.2 copy-start.1
  49.5 8.6 %copy-start.2 = (bf16[256,3072]{1,0:T(8,128)(2,1)S(1)}, bf16[256,3072]{1,0:T(8,128)(2,1)}, u32[]{:S(2)}) copy-start(bf16[256,3072]{1,0:T(8,128)(2,1)} %copy-done.1) | copy-start | bytes 4718596
  49.5 8.6 %copy-start.4 = (bf16[3072,128]{1,0:T(8,128)(2,1)S(1)}, bf16[3072,128]{1,0:T(8,128)(2,1)}, u32[]{:S(2)}) copy-start(bf16[3072,128]{1,0:T(8,128)(2,1)} %param.26) | copy-start | bytes 2359300
  49.5 21.7 %copy-start.11 = (bf16[1,3,384]{2,1,0:T(4,128)(2,1)S(1)}, bf16[1,3,384]{2,1,0:T(4,128)(2,1)}, u32[]{:S(2)}) copy-start(bf16[1,3,384]{2,1,0:T(4,128)(2,1)} %param.37) | copy-start | bytes 6916
  53.8 18.6 %copy-start.10 = (bf16[1,3,512]{2,1,0:T(4,128)(2,1)S(1)}, bf16[1,3,512]{2,1,0:T(4,128)(2,1)}, u32[]{:S(2)}) copy-start(bf16[1,3,512]{2,1,0:T(4,128)(2,1)} %param.38) | copy-start | bytes 9220
  53.9 17.3 %collective-permute-start.2 = (bf16[3,384]{1,0:T(4,128)(2,1)S(1)}, bf16[3,384]{1,0:T(4,128)(2,1)S(1)}, u32[]{:S(2)}, u32[]{:S(2)}) collective-permute-start(bf16[3,384]{1,0:T(4,128)(2,1)S(1)} %slice_bitcast_fusion.73), channel_id=1, source_target_pairs={{0,8},{8,16},{16,24},{24,32},{32,40},{40,48},{48,56},{56,64},{64,7... | collective-permute-start | bytes 6920 | tf_op jit(solution)/shard_map/ppermute | solution.py:19
  68.4 6.2 %copy-start.12 = (f32[3]{0:T(128)}, f32[3]{0:T(128)S(1)}, u32[]{:S(2)}) copy-start(f32[3]{0:T(128)S(1)} %exp.54) | copy-start | bytes 40
  68.4 4.0 %collective-permute-start.3 = (bf16[3,512]{1,0:T(4,128)(2,1)S(1)}, bf16[3,512]{1,0:T(4,128)(2,1)S(1)}, u32[]{:S(2)}, u32[]{:S(2)}) collective-permute-start(bf16[3,512]{1,0:T(4,128)(2,1)S(1)} %slice.510), channel_id=1, source_target_pairs={{0,8},{8,16},{16,24},{24,32},{32,40},{40,48},{48,56},{56,64},{64,7... | collective-permute-start | bytes 9224 | tf_op jit(solution)/shard_map/ppermute | solution.py:19
  75.7 26.1 %all-to-all-start = ((f32[32,3,5,256]{3,1,2,0:T(4,128)}), f32[32,3,5,256]{3,1,2,0:T(4,128)}, u32[]{:S(2)}, u32[]{:S(2)}) async-start(f32[32,3,5,256]{3,1,2,0:T(4,128)} %pad_maximum_fusion), calls=%async_computation | async-start | bytes 1310720 | tf_op jit(solution)/shard_map/all_to_all | solution.py:155
  86.4 131.6 %all-gather.7.cloned.1.call-start = ((), (), s32[]{:S(2)}) async-start(), calls=%async_computation.4 | async-start | bytes 4325376 | tf_op jit(solution)/shard_map/all_gather | solution.py:124
  89.1 3.2 copy-start.5
  89.1 3.2 collective-permute-start.1
  124.7 18.9 %all-to-all-start.1 = ((f32[32,3,4,256]{3,2,1,0:T(4,128)}), f32[32,3,4,256]{3,2,1,0:T(4,128)}, u32[]{:S(2)}, u32[]{:S(2)}) async-start(f32[32,3,4,256]{3,2,1,0:T(4,128)} %copy.77), calls=%async_computation.1 | async-start | bytes 786432 | tf_op jit(solution)/shard_map/all_to_all | solution.py:162
  131.7 190.3 %reduce-scatter.2.cloned.1.call-start = ((), (), s32[]{:S(2)}) async-start(), calls=%async_computation.5 | async-start | bytes 3932160 | tf_op jit(solution)/shard_map/reduce_scatter | solution.py:204
  156.0 66.6 %copy-start.7 = (bf16[256,2,64]{2,0,1:T(8,128)(2,1)S(1)}, bf16[256,2,64]{2,0,1:T(8,128)(2,1)}, u32[]{:S(2)}) copy-start(bf16[256,2,64]{2,0,1:T(8,128)(2,1)} %get-tuple-element.49) | copy-start | bytes 196612
  156.0 66.6 %copy-start.8 = (bf16[256,2,64]{2,0,1:T(8,128)(2,1)S(1)}, bf16[256,2,64]{2,0,1:T(8,128)(2,1)}, u32[]{:S(2)}) copy-start(bf16[256,2,64]{2,0,1:T(8,128)(2,1)} %get-tuple-element.50) | copy-start | bytes 196612
  274.9 2.8 copy-start.6
  274.9 3.5 %copy-start.3 = (f32[3,128,256]{2,1,0:T(8,128)S(1)}, f32[3,128,256]{2,1,0:T(8,128)}, u32[]{:S(2)}) copy-start(f32[3,128,256]{2,1,0:T(8,128)} %reshape.277) | copy-start | bytes 1179652
  274.9 3.5 %copy-start.13 = (f32[3]{0:T(128)S(1)}, f32[3]{0:T(128)}, u32[]{:S(2)}) copy-start(f32[3]{0:T(128)} %copy-done.12) | copy-start | bytes 40
Sparse Core Ops, SparseCore 0:
  9.8 32.8 all-gather.8
  45.2 86.1 all-gather.4
  133.8 84.1 all-gather.6
  277.7 44.2 reduce-scatter.1
where the time goes:
time: 332 us; the launch traced here: 331 us
  waiting for transfers between devices  125 us (38%)
  other arithmetic  69.1 us (21%)
  matrix products  55.4 us (17%)
  local copies, waits for them, and re-layouts  28.8 us (9%)
  starting transfers between devices  27.1 us (8%)
  between operations  14.9 us (4%)
  blocking collectives  9.8 us (3%)
    all_gather x1, waiting for transfers between devices, shards(): new_all = lax.all_gather(paired(kv_block), 'seq', axis=0, tiled=True)  62 us
    reduce_scatter x1, waiting for transfers between devices, shards(): summed = lax.psum_scatter(term, 'mp', scatter_dimension=1, tiled=True)  42.8 us
    unnamed x31, other arithmetic  18.3 us
    dot_general x1, matrix products, shards(): jnp.einsum('qhd,kd->hqk', query, piece[:, :HD], preferred_element_type=jn...  17.3 us
    dot_general x1, matrix products, shards(): jnp.einsum('hqk,kd->hqd', weights.astype(jnp.bfloat16), piece[:, HD:2 * H...  17.2 us
    reduce_sum x1, other arithmetic, shards(): total = jnp.sum(weights, axis=-1)  15.7 us
    or x1, other arithmetic, shards(): slot_ok[None, :]  15.6 us
    unnamed x37, local copies, waits for them, and re-layouts  10.8 us
  transfers between devices with their start and end apart: 10, of which 6 were waited for; matrix products, arithmetic and copies ran while one was open for 27% of the time, Pallas kernels for 0%

commit v1 on v0

--- a/solution.py
+++ b/solution.py
@@ -121,7 +121,15 @@
         )
 
     cache_all = lax.all_gather(paired(cache[0]), "seq", axis=0, tiled=True)
-    new_all = lax.all_gather(paired(kv_block), "seq", axis=0, tiled=True)
+    new_all = jnp.concatenate(
+        lax.all_to_all(
+            jnp.stack(lax.axis_size("seq") * [paired(kv_block)], axis=0),
+            axis_name="seq",
+            split_axis=0,
+            concat_axis=0,
+        ),
+        axis=0,
+    )
     inner = jnp.einsum("td,dkc->tkc", normed, w_inner, preferred_element_type=jnp.float32).astype(
         jnp.bfloat16
     )

time: 332 us -> 372 us (1.12)
  waiting for transfers between devices: 125 us -> 162 us
  local copies, waits for them, and re-layouts: 28.8 us -> 33 us
    all_gather x1 -> x0, waiting for transfers between devices: 62 us -> none  [shards(): new_all = lax.all_gather(paired(kv_block), 'seq', axis=0, tiled=True)]
    all_gather x1, waiting for transfers between devices: 0.02 us -> 45 us  [shards(): cache_all = lax.all_gather(paired(cache[0]), 'seq', axis=0, tiled=True)]
    all_to_all x0 -> x1, waiting for transfers between devices: none -> 23.6 us  [shards(): lax.all_to_all(jnp.stack(lax.axis_size('seq') * [paired(kv_block)], axis=...]
    all_gather x1, waiting for transfers between devices: 8.26 us -> 31.7 us  [shards(): whole = lax.all_gather(own_rows, 'mp', axis=1, tiled=True)]
    all_to_all x0 -> x1, starting transfers between devices: none -> 5.08 us  [shards(): lax.all_to_all(jnp.stack(lax.axis_size('seq') * [paired(kv_block)], axis=...]
    concatenate x1, local copies, waits for them, and re-layouts: 4.57 us -> 0.43 us  [shards(): piece = jnp.concatenate([cache_all, new_all], axis=0)]
    unnamed x37 -> x49, local copies, waits for them, and re-layouts: 10.8 us -> 13.9 us
  transfers between devices with their start and end apart: 10 -> 10, of which waited for: 6 -> 8; matrix products, arithmetic and copies ran while one was open for 27% -> 20% of each run, Pallas kernels for 0% -> 0%
where the time goes in v1:
time: 372 us; the launch traced here: 371 us
  waiting for transfers between devices  162 us (44%)
  other arithmetic  67.8 us (18%)
  matrix products  52.2 us (14%)
  local copies, waits for them, and re-layouts  33 us (9%)
  starting transfers between devices  29.1 us (8%)
  between operations  16.8 us (5%)
  blocking collectives  9.36 us (3%)
    all_gather x1, waiting for transfers between devices, shards(): cache_all = lax.all_gather(paired(cache[0]), 'seq', axis=0, tiled=True)  45 us
    reduce_scatter x1, waiting for transfers between devices, shards(): summed = lax.psum_scatter(term, 'mp', scatter_dimension=1, tiled=True)  41.4 us
    all_gather x1, waiting for transfers between devices, shards(): whole = lax.all_gather(own_rows, 'mp', axis=1, tiled=True)  31.7 us
    all_to_all x1, waiting for transfers between devices, shards(): lax.all_to_all(jnp.stack(lax.axis_size('seq') * [paired(kv_block)], axis=...  23.6 us
    unnamed x31, other arithmetic  18.3 us
    dot_general x1, matrix products, shards(): jnp.einsum('hqk,kd->hqd', weights.astype(jnp.bfloat16), piece[:, HD:2 * H...  17.4 us
    dot_general x1, matrix products, shards(): jnp.einsum('qhd,kd->hqk', query, piece[:, :HD], preferred_element_type=jn...  17.2 us
    reduce_sum x1, other arithmetic, shards(): total = jnp.sum(weights, axis=-1)  15.7 us
  transfers between devices with their start and end apart: 10, of which 8 were waited for; matrix products, arithmetic and copies ran while one was open for 20% of the time, Pallas kernels for 0%

profile of v1, /device:TPU:1, one launch (start us, length us, event | category | flops | bytes accessed | tf_op | source)
XLA Modules:
  0.0 370.7 jit_solution(8449012528934889817)
XLA Ops:
  10.1 0.9 convert_reduce_fusion.3
  11.8 31.7 %all-gather.6.cloned.1.call-done = bf16[1,256,3072]{2,1,0:T(8,128)(2,1)} async-done(((bf16[1,256,768]{2,1,0:T(8,128)(2,1)}), bf16[1,256,3072]{2,1,0:T(8,128)(2,1)}) %all-gather.6.cloned.1.call-update) | async-done | bytes 1572880 | tf_op jit(solution)/shard_map/all_gather | solution.py:94
  43.5 1.9 fusion.9
  45.5 1.9 fusion.11
  47.5 1.4 fusion.13
  50.3 0.9 reduce-window.6
  51.8 2.0 convolution_convert_fusion
  53.8 3.1 collective-permute-start.2
  57.0 9.4 %all_gather.11 = bf16[256,512]{1,0:T(8,128)(2,1)S(1)} all-gather(bf16[256,128]{1,0:T(8,128)(2,1)S(1)} %convolution_convert_fusion), channel_id=1, replica_groups=mesh['seq'=32,'mp'=4,'req'=2] {'mp'}, dimensions={1}, use_global_device_ids=true | all-gather | bytes 327680 | tf_op jit(solution)/shard_map/all_gather | solution.py:110
  66.4 3.1 collective-permute-start.3
  69.8 0.9 copy.74
  71.2 1.5 fusion.45
  73.0 1.0 pad_maximum_fusion
  74.0 10.5 %all-to-all-start.1 = ((f32[32,3,5,256]{3,1,2,0:T(4,128)}), f32[32,3,5,256]{3,1,2,0:T(4,128)}, u32[]{:S(2)}, u32[]{:S(2)}) async-start(f32[32,3,5,256]{3,1,2,0:T(4,128)} %pad_maximum_fusion), calls=%async_computation.1 | async-start | bytes 1310720 | tf_op jit(solution)/shard_map/all_to_all | solution.py:163
  86.9 1.1 collective-permute-done
  88.6 10.6 %all-to-all-done.1 = f32[32,3,5,256]{3,1,2,0:T(4,128)} async-done(((f32[32,3,5,256]{3,1,2,0:T(4,128)}), f32[32,3,5,256]{3,1,2,0:T(4,128)}, u32[]{:S(2)}, u32[]{:S(2)}) %all-to-all-start.1) | async-done | bytes 491552 | tf_op jit(solution)/shard_map/all_to_all | solution.py:163
  99.2 1.0 slice_bitcast_fusion.11
  100.2 0.9 slice_bitcast_fusion.30
  120.2 1.9 copy.79
  122.1 6.8 %all-to-all-start.2 = ((f32[32,3,4,256]{3,2,1,0:T(4,128)}), f32[32,3,4,256]{3,2,1,0:T(4,128)}, u32[]{:S(2)}, u32[]{:S(2)}) async-start(f32[32,3,4,256]{3,2,1,0:T(4,128)} %copy.79), calls=%async_computation.2 | async-start | bytes 786432 | tf_op jit(solution)/shard_map/all_to_all | solution.py:170
  128.9 2.3 fusion.90
  131.6 3.5 collective-permute-done.1
  135.2 4.9 %all-to-all-done.2 = f32[32,3,4,256]{3,2,1,0:T(4,128)} async-done(((f32[32,3,4,256]{3,2,1,0:T(4,128)}), f32[32,3,4,256]{3,2,1,0:T(4,128)}, u32[]{:S(2)}, u32[]{:S(2)}) %all-to-all-start.2) | async-done | bytes 393248 | tf_op jit(solution)/shard_map/all_to_all | solution.py:170
  140.1 2.4 stack.132
  142.5 5.1 %all-to-all-start = ((bf16[32,256,256]{1,2,0:T(8,128)(2,1)}), bf16[32,256,256]{1,2,0:T(8,128)(2,1)}, u32[]{:S(2)}, u32[]{:S(2)}) async-start(bf16[32,256,256]{1,2,0:T(8,128)(2,1)} %stack.132), calls=%async_computation | async-start | bytes 8388608 | tf_op jit(solution)/shard_map/all_to_all | solution.py:125
  148.6 1.2 multiply_cosine_fusion
  149.8 15.5 %and_or_fusion = pred[256,16384]{0,1:T(8,128)(4,1)} fusion(s32[256]{0:T(256)S(1)} %iota_add_fusion.1, s32[16384]{0:T(1024)S(1)} %iota_add_fusion, pred[16384]{0:T(1024)(128)(4,1)S(1)} %get-tuple-element.103, pred[16384]{0:T(1024)(128)(4,1)S(1)} %get-tuple-element.104), kind=kLoop, calls=%fused_computation.7 | loop fusion | flops 12582912 | bytes 4293632 | tf_op jit(solution)/shard_map/or | solution.py:193
  166.8 1.0 copy.88
  167.8 1.9 copy.81
  169.8 1.7 copy.87
  171.5 1.8 subtract_convert_fusion
  173.7 1.8 copy.80
  175.5 1.9 reshape.294
  177.4 1.5 convolution_multiply_fusion
  178.9 2.5 multiply_reduce_fusion
  181.6 45.0 %all-gather.4.cloned.1.call-done = bf16[8192,256]{0,1:T(8,128)(2,1)} async-done(((bf16[256,256]{0,1:T(8,128)(2,1)}), bf16[8192,256]{0,1:T(8,128)(2,1)}) %all-gather.4.cloned.1.call-update) | async-done | bytes 4194320 | tf_op jit(solution)/shard_map/all_gather | solution.py:123
  226.6 4.6 %constant_dynamic-update-slice_fusion.1 = bf16[16384,256]{0,1:T(8,128)(2,1)} fusion(bf16[8192,256]{0,1:T(8,128)(2,1)} %all-gather.4.cloned.1.call-done), kind=kLoop, calls=%fused_computation.102 | loop fusion | bytes 8388608
  231.2 23.6 %all-to-all-done = bf16[32,256,256]{1,2,0:T(8,128)(2,1)} async-done(((bf16[32,256,256]{1,2,0:T(8,128)(2,1)}), bf16[32,256,256]{1,2,0:T(8,128)(2,1)}, u32[]{:S(2)}, u32[]{:S(2)}) %all-to-all-start) | async-done | bytes 4194336 | tf_op jit(solution)/shard_map/all_to_all | solution.py:125
  254.8 2.8 copy.90
  257.6 1.8 copy-done.4
  259.9 3.2 copy-done.5
  263.1 17.2 %fusion = (f32[2,256]{1,0:T(2,128)S(1)}, f32[16384,256,2]{1,0,2:T(8,128)}) fusion(pred[256,16384]{0,1:T(8,128)(4,1)} %and_or_fusion, bf16[256,2,64]{2,0,1:T(8,128)(2,1)S(1)} %copy-done.11, bf16[256,2,64]{2,0,1:T(8,128)(2,1)S(1)} %copy-done.10, bf16[16384,256]{0,1:T(8,128)(2,1)} %copy-done.5), kind=kOutput, calls=%fused_computation.2 | convolution fusion | flops 2172911104 | bytes 42076160 | tf_op jit(solution)/shard_map/qhd,kd->hqk/dot_general | solution.py:195
  280.4 15.7 %fusion.1 = f32[2,256]{1,0:T(2,128)S(1)} fusion(f32[16384,256,2]{1,0,2:T(8,128)} %get-tuple-element.98, f32[2,256]{1,0:T(2,128)S(1)} %broadcast_maximum_fusion, pred[256,16384]{0,1:T(8,128)(4,1)} %and_or_fusion), kind=kLoop, calls=%fused_computation.3 | loop fusion | flops 41942528 | bytes 37752832 | tf_op jit(solution)/shard_map/reduce_sum | solution.py:200
  296.1 17.4 %fusion.27 = bf16[256,2,128]{0,2,1:T(8,128)(2,1)S(1)} fusion(f32[16384,256,2]{1,0,2:T(8,128)} %get-tuple-element.98, f32[2,256]{1,0:T(2,128)S(1)} %broadcast_maximum_fusion, pred[256,16384]{0,1:T(8,128)(4,1)} %and_or_fusion, bf16[16384,256]{0,1:T(8,128)(2,1)} %copy-done.5, f32[256,2]{0,1:T(2,128)S(1)} %bitcast.370), kind=kOutput, calls=%fused_computation.30 | convolution fusion | flops 2189557760 | bytes 42078208 | tf_op jit(solution)/shard_map/hqk,kd->hqd/dot_general | solution.py:201
  313.5 2.0 fusion.92
  315.5 2.7 convolution_add_fusion
  319.9 41.4 %reduce-scatter.2.cloned.1.call-done = f32[256,768]{1,0:T(8,128)} async-done(((f32[256,3072]{1,0:T(8,128)}), f32[256,768]{1,0:T(8,128)}) %reduce-scatter.2.cloned.1.call-update) | async-done | bytes 786448 | tf_op jit(solution)/shard_map/reduce_scatter | solution.py:212
  361.3 2.0 fusion.40
  (148 shorter events, 32.8 us)
Async XLA Ops:
  8.0 307.5 %copy-start = (bf16[384,3072]{1,0:T(8,128)(2,1)S(1)}, bf16[384,3072]{1,0:T(8,128)(2,1)}, u32[]{:S(2)}) copy-start(bf16[384,3072]{1,0:T(8,128)(2,1)} %param.34) | copy-start | bytes 7077892
  8.0 35.5 %all-gather.6.cloned.1.call-start = ((), (), s32[]{:S(2)}) async-start(), calls=%async_computation.6 | async-start | bytes 1966080 | tf_op jit(solution)/shard_map/all_gather | solution.py:94
  43.5 3.9 %copy-start.20 = (bf16[3072,2,384]{2,1,0:T(2,128)(2,1)S(1)}, bf16[3072,2,384]{2,1,0:T(2,128)(2,1)}, u32[]{:S(2)}) copy-start(bf16[3072,2,384]{2,1,0:T(2,128)(2,1)} %param.25) | copy-start | bytes 14155780
  47.4 2.3 copy-start.1
  47.4 2.3 copy-start.13
  47.4 2.3 copy-start.19
  47.5 4.4 %copy-start.7 = (bf16[3072,128]{1,0:T(8,128)(2,1)S(1)}, bf16[3072,128]{1,0:T(8,128)(2,1)}, u32[]{:S(2)}) copy-start(bf16[3072,128]{1,0:T(8,128)(2,1)} %param.26) | copy-start | bytes 2359300
  48.9 20.6 %copy-start.15 = (bf16[1,3,384]{2,1,0:T(4,128)(2,1)S(1)}, bf16[1,3,384]{2,1,0:T(4,128)(2,1)}, u32[]{:S(2)}) copy-start(bf16[1,3,384]{2,1,0:T(4,128)(2,1)} %param.37) | copy-start | bytes 6916
  48.9 21.8 %copy-start.14 = (bf16[1,3,512]{2,1,0:T(4,128)(2,1)S(1)}, bf16[1,3,512]{2,1,0:T(4,128)(2,1)}, u32[]{:S(2)}) copy-start(bf16[1,3,512]{2,1,0:T(4,128)(2,1)} %param.38) | copy-start | bytes 9220
  53.8 15.7 %collective-permute-start.2 = (bf16[3,384]{1,0:T(4,128)(2,1)S(1)}, bf16[3,384]{1,0:T(4,128)(2,1)S(1)}, u32[]{:S(2)}, u32[]{:S(2)}) collective-permute-start(bf16[3,384]{1,0:T(4,128)(2,1)S(1)} %slice_bitcast_fusion.73), channel_id=1, source_target_pairs={{0,8},{8,16},{16,24},{24,32},{32,40},{40,48},{48,56},{56,64},{64,7... | collective-permute-start | bytes 6920 | tf_op jit(solution)/shard_map/ppermute | solution.py:19
  66.3 6.6 %copy-start.16 = (f32[3]{0:T(128)}, f32[3]{0:T(128)S(1)}, u32[]{:S(2)}) copy-start(f32[3]{0:T(128)S(1)} %exp.54) | copy-start | bytes 40
  66.4 4.4 %collective-permute-start.3 = (bf16[3,512]{1,0:T(4,128)(2,1)S(1)}, bf16[3,512]{1,0:T(4,128)(2,1)S(1)}, u32[]{:S(2)}, u32[]{:S(2)}) collective-permute-start(bf16[3,512]{1,0:T(4,128)(2,1)S(1)} %slice.510), channel_id=1, source_target_pairs={{0,8},{8,16},{16,24},{24,32},{32,40},{40,48},{48,56},{56,64},{64,7... | collective-permute-start | bytes 9224 | tf_op jit(solution)/shard_map/ppermute | solution.py:19
  70.7 13.9 %copy-start.12 = (bf16[1,256,128]{2,1,0:T(8,128)(2,1)S(1)}, bf16[1,256,128]{2,1,0:T(8,128)(2,1)}, u32[]{:S(2)}) copy-start(bf16[1,256,128]{2,1,0:T(8,128)(2,1)} %param.35) | copy-start | bytes 196612
  74.0 25.2 %all-to-all-start.1 = ((f32[32,3,5,256]{3,1,2,0:T(4,128)}), f32[32,3,5,256]{3,1,2,0:T(4,128)}, u32[]{:S(2)}, u32[]{:S(2)}) async-start(f32[32,3,5,256]{3,1,2,0:T(4,128)} %pad_maximum_fusion), calls=%async_computation.1 | async-start | bytes 1310720 | tf_op jit(solution)/shard_map/all_to_all | solution.py:163
  84.6 142.1 %all-gather.4.cloned.1.call-start = ((), (), s32[]{:S(2)}) async-start(), calls=%async_computation.4 | async-start | bytes 4325376 | tf_op jit(solution)/shard_map/all_gather | solution.py:123
  84.7 3.2 collective-permute-start
  122.1 18.0 %all-to-all-start.2 = ((f32[32,3,4,256]{3,2,1,0:T(4,128)}), f32[32,3,4,256]{3,2,1,0:T(4,128)}, u32[]{:S(2)}, u32[]{:S(2)}) async-start(f32[32,3,4,256]{3,2,1,0:T(4,128)} %copy.79), calls=%async_computation.2 | async-start | bytes 786432 | tf_op jit(solution)/shard_map/all_to_all | solution.py:170
  131.5 3.6 copy-start.8
  131.5 3.6 collective-permute-start.1
  142.5 5.3 %copy-start.18 = (bf16[384]{0:T(512)(128)(2,1)S(1)}, bf16[384]{0:T(512)(128)(2,1)}, u32[]{:S(2)}) copy-start(bf16[384]{0:T(512)(128)(2,1)} %param.33) | copy-start | bytes 2308
  142.5 112.3 %all-to-all-start = ((bf16[32,256,256]{1,2,0:T(8,128)(2,1)}), bf16[32,256,256]{1,2,0:T(8,128)(2,1)}, u32[]{:S(2)}, u32[]{:S(2)}) async-start(bf16[32,256,256]{1,2,0:T(8,128)(2,1)} %stack.132), calls=%async_computation | async-start | bytes 8388608 | tf_op jit(solution)/shard_map/all_to_all | solution.py:125
  147.6 213.7 %reduce-scatter.2.cloned.1.call-start = ((), (), s32[]{:S(2)}) async-start(), calls=%async_computation.5 | async-start | bytes 3932160 | tf_op jit(solution)/shard_map/reduce_scatter | solution.py:212
  147.8 17.5 %copy-start.2 = (bf16[256,3072]{1,0:T(8,128)(2,1)S(1)}, bf16[256,3072]{1,0:T(8,128)(2,1)}, u32[]{:S(2)}) copy-start(bf16[256,3072]{1,0:T(8,128)(2,1)} %copy-done.1) | copy-start | bytes 4718596
  147.8 17.5 %copy-start.6 = (bf16[3072,256]{1,0:T(8,128)(2,1)S(1)}, bf16[3072,256]{1,0:T(8,128)(2,1)}, u32[]{:S(2)}) copy-start(bf16[3072,256]{1,0:T(8,128)(2,1)} %param.22) | copy-start | bytes 4718596
  254.8 4.6 %copy-start.4 = (bf16[16384,256]{0,1:T(8,128)(2,1)S(1)}, bf16[16384,256]{0,1:T(8,128)(2,1)}, u32[]{:S(2)}) copy-start(bf16[16384,256]{0,1:T(8,128)(2,1)} %constant_dynamic-update-slice_fusion.1) | copy-start | bytes 25165828
  259.4 3.7 copy-start.10
  259.4 3.7 copy-start.11
  259.9 3.3 copy-start.5
  315.5 2.8 copy-start.9
  315.5 3.5 copy-start.3
  315.5 3.5 copy-start.17
Sparse Core Ops, SparseCore 0:
  10.7 32.8 all-gather.5
  318.4 42.8 reduce-scatter.1
Sparse Core Ops, SparseCore 1:
  88.7 137.9 all-gather.3
